TPU v7x, 128 devices: a whole 4x4x4 slice. The times are simulated.
128 devices in a mesh: row: 64 (over z, y, x), pan: 2 (over core).
Axes of the slice: x: 4, y: 4, z: 4, core: 2. Of those that a mesh axis runs over, the one named last changes fastest.
Arguments:
- right_side: float32 [256, 65536], P(None, 'row'), may hold values from -6 to 6
- initial_guess: float32 [256, 65536], P(None, ('row', 'pan')), may hold values from -6 to 6
- v_factor: float32 [128, 128, 16, 512], P('row', None, 'pan'), may hold values from -0.25 to 0.25
- u_factor: float32 [128, 128, 16, 512], P('row', None, 'pan'), may hold values from -0.125 to 0.125
- tile_ranks: int32 [128, 128], P(None, 'row'), may hold values from 0 to 16
- diag_block: float32 [65536, 512], P(('row', 'pan'))
- diag_inverse: float32 [65536, 512], P(('row', 'pan'))
Outputs:
- solution: float32 [256, 65536], P(None, ('row', 'pan'))
- residual: float32 [256, 65536], P(None, ('row', 'pan'))
Inputs may be any that keep to these rules, and one draw needn't show every extreme that they name: `tile_ranks`: columns of a tile's factors from its rank on are ignored, as is the low-rank part of tile (i, i).
All inputs are finite; a program needn't handle non-finite values.
Results may differ from a plain program's by a relative error of at most 0.00017.
Values sent between devices are 32-bit elements; how exact they have to be, the bound alone decides.
A program may use at most 64 MiB of HBM per device.

v0:
```python
import jax
import jax.numpy as jnp
from jax import lax
from jax.sharding import PartitionSpec as P

ITERS = 2


def on_device(right_side, initial_guess, v_factor, u_factor, tile_ranks, diag_block, diag_inverse):
    highest = lax.Precision.HIGHEST
    pan_index = lax.axis_index("pan")
    row_index = lax.axis_index("row")
    tile_rows = v_factor.shape[0]
    tile_count = v_factor.shape[1]
    part_rank = v_factor.shape[2]
    tile_width = v_factor.shape[3]
    rhs_count = right_side.shape[0]
    own_rows = diag_block.shape[0]
    row_start = pan_index * own_rows
    tile_slot = row_start // tile_width
    components = pan_index * part_rank + jnp.arange(part_rank, dtype=jnp.int32)
    own_columns = row_index * tile_rows + jnp.arange(tile_rows, dtype=jnp.int32)
    tile_index = jnp.arange(tile_count, dtype=jnp.int32)
    off_diagonal = tile_index[:, None] != own_columns[None, :]
    rank_mask = (
        (components[None, None, :] < tile_ranks[:, :, None]) & off_diagonal[:, :, None]
    ).astype(jnp.float32)
    iterate_rows = initial_guess
    residual = initial_guess
    for iteration in range(ITERS):
        guess_full = lax.all_gather(iterate_rows, "pan", axis=1, tiled=True)
        guess_tiles = guess_full.reshape(rhs_count, tile_rows, tile_width)
        projected = jnp.einsum("cikb,rcb->ickr", v_factor, guess_tiles, precision=highest)
        projected = projected * rank_mask[:, :, :, None]
        received = lax.all_to_all(projected, "row", split_axis=0, concat_axis=1, tiled=True)
        low_rank = jnp.einsum("ickm,ickr->rim", u_factor, received, precision=highest)
        low_rank = low_rank.reshape(rhs_count, tile_rows * tile_width)
        guess_tile = lax.dynamic_slice_in_dim(guess_full, tile_slot * tile_width, tile_width, 1)
        dense_part = jnp.einsum("rb,mb->rm", guess_tile, diag_block, precision=highest)
        low_rows = lax.psum_scatter(low_rank, "pan", scatter_dimension=1, tiled=True)
        rhs_rows = lax.dynamic_slice_in_dim(right_side, row_start, own_rows, 1)
        residual = rhs_rows - (dense_part + low_rows)
        residual_full = lax.all_gather(residual, "pan", axis=1, tiled=True)
        residual_tile = lax.dynamic_slice_in_dim(
            residual_full, tile_slot * tile_width, tile_width, 1
        )
        update = jnp.einsum("rb,mb->rm", residual_tile, diag_inverse, precision=highest)
        iterate_rows = iterate_rows + update
    return (iterate_rows, residual)


def solution(mesh):
    placed = (
        P(None, "row"),
        P(None, ("row", "pan")),
        P("row", None, "pan", None),
        P("row", None, "pan", None),
        P(None, "row"),
        P(("row", "pan"), None),
        P(("row", "pan"), None),
    )
    return jax.shard_map(
        on_device,
        mesh=mesh,
        in_specs=placed,
        out_specs=(P(None, ("row", "pan")), P(None, ("row", "pan"))),
        check_vma=False,
    )
```

profile of v0, /device:TPU:1, one launch (start us, length us, event | category | flops | bytes accessed | tf_op | source)
XLA Modules:
  0.0 225.6 jit_solution(9807114171824869542)
XLA Ops:
  7.2 2.1 copy.33
  9.4 0.0 reduce-scatter.3.cloned.1.call-start
  9.4 0.1 iota_compare_fusion
  9.5 0.8 and_convert_fusion
  10.3 15.4 %all-gather.5.cloned.1.call-done = f32[256,1024]{0,1:T(8,128)} async-done(((f32[256,512]{0,1:T(8,128)}), f32[256,1024]{0,1:T(8,128)}) %all-gather.5.cloned.1.call-update) | async-done | bytes 1048592 | tf_op jit(solution)/shard_map/all_gather | solution.py:31
  25.7 12.3 %bitcast_multiply_fusion.1 = f32[128,2,8,256]{0,3,2,1:T(8,128)} fusion(f32[256,2,512,1]{0,2,3,1:T(8,128)} %bitcast.45, f32[2,128,8,512]{3,2,1,0:T(8,128)} %param.9, f32[128,2,8]{0,2,1:T(8,128)S(1)} %and_convert_fusion), kind=kOutput, calls=%fused_computation.5 | convolution fusion | flops 3221749760 | bytes 7348224 | tf_op jit(solution)/shard_map/cikb,rcb->ickr/dot_general | solution.py:33
  38.0 2.2 copy.36
  40.2 39.2 %all_to_all.36 = f32[128,2,8,256]{3,2,1,0:T(8,128)S(1)} all-to-all(f32[128,2,8,256]{3,2,1,0:T(8,128)S(1)} %copy.36), channel_id=1, replica_groups=mesh['row'=64,'pan'=2] {'row'}, dimensions={0} | all-to-all | bytes 4194304 | tf_op jit(solution)/shard_map/all_to_all | solution.py:35
  79.5 0.2 copy.37
  79.7 2.0 copy-done.5
  81.7 3.8 %convolution_bitcast_fusion.1 = f32[256,2,512]{2,0,1:T(8,128)S(1)} fusion(f32[2,128,8,256]{3,2,1,0:T(8,128)S(1)} %bitcast.46, f32[2,128,8,512]{3,2,1,0:T(8,128)S(1)} %copy-done.5), kind=kOutput, calls=%fused_computation.7 | convolution fusion | flops 3221225472 | bytes 7340032 | tf_op jit(solution)/shard_map/ickm,ickr->rim/dot_general | solution.py:36
  85.5 0.3 copy.38
  85.9 1.3 copy.39
  87.3 9.3 %reduce-scatter.3.cloned.1.call-done = f32[256,512]{1,0:T(8,128)} async-done(((f32[256,1024]{1,0:T(8,128)}), f32[256,512]{1,0:T(8,128)}) %reduce-scatter.3.cloned.1.call-update) | async-done | bytes 524304 | tf_op jit(solution)/shard_map/reduce_scatter | solution.py:40
  96.6 3.9 %fusion.8 = f32[256,512]{1,0:T(8,128)} fusion(f32[256,512]{1,0:T(8,128)} %reduce-scatter.3.cloned.1.call-done, f32[512,512]{1,0:T(8,128)S(1)} %copy-done, f32[256,1024]{0,1:T(8,128)S(1)} %copy-done.4, s32[]{:T(128)S(6)} %select_n.17, f32[256,1024]{1,0:T(8,128)} %param.7, s32[]{:T(128)S(6)} %select_n.15), kind=kOutput, calls=%fused_computation.12 | convolution fusion | flops 805568512 | bytes 3145736 | tf_op jit(solution)/shard_map/rb,mb->rm/dot_general | solution.py:39
  100.5 0.0 all-gather.9.cloned.1.call-start
  100.6 13.2 %all-gather.7.cloned.1.call-done = f32[256,1024]{1,0:T(8,128)} async-done(((f32[256,512]{1,0:T(8,128)}), f32[256,1024]{1,0:T(8,128)}) %all-gather.7.cloned.1.call-update) | async-done | bytes 1048592 | tf_op jit(solution)/shard_map/all_gather | solution.py:43
  113.7 3.1 %convolution_add_fusion.2 = f32[256,512]{1,0:T(8,128)} fusion(f32[256,512]{1,0:T(8,128)} %param.8, f32[512,512]{1,0:T(8,128)S(1)} %copy-done.2, f32[256,1024]{1,0:T(8,128)} %all-gather.7.cloned.1.call-done, s32[]{:T(128)S(6)} %select_n.17), kind=kOutput, calls=%fused_computation.10 | convolution fusion | flops 805437440 | bytes 2621444 | tf_op jit(solution)/shard_map/rb,mb->rm/dot_general | solution.py:47
  116.8 0.3 reduce-scatter.5.cloned.1.call-start
  117.1 13.0 %all-gather.9.cloned.1.call-done = f32[256,1024]{1,0:T(8,128)} async-done(((f32[256,512]{1,0:T(8,128)}), f32[256,1024]{1,0:T(8,128)}) %all-gather.9.cloned.1.call-update) | async-done | bytes 1048592 | tf_op jit(solution)/shard_map/all_gather | solution.py:31
  130.0 2.1 reshape.49
  132.1 9.3 %bitcast_multiply_fusion = f32[128,2,8,256]{0,3,2,1:T(8,128)} fusion(f32[2,128,8,512]{3,2,1,0:T(8,128)} %param.9, f32[256,2,512,1]{2,1,0,3:T(2,128)S(1)} %bitcast.44, f32[128,2,8]{0,2,1:T(8,128)S(1)} %and_convert_fusion), kind=kOutput, calls=%fused_computation.4 | convolution fusion | flops 3221749760 | bytes 7348224 | tf_op jit(solution)/shard_map/cikb,rcb->ickr/dot_general | solution.py:33
  141.4 2.2 copy.42
  143.7 39.2 %all_to_all.37 = f32[128,2,8,256]{3,2,1,0:T(8,128)S(1)} all-to-all(f32[128,2,8,256]{3,2,1,0:T(8,128)S(1)} %copy.42), channel_id=1, replica_groups=mesh['row'=64,'pan'=2] {'row'}, dimensions={0} | all-to-all | bytes 4194304 | tf_op jit(solution)/shard_map/all_to_all | solution.py:35
  182.9 0.2 copy.43
  183.1 2.0 copy-done.6
  185.1 3.8 %convolution_bitcast_fusion = f32[2,32,8,512]{3,2,1,0:T(8,128)S(1)} fusion(f32[2,128,8,256]{3,2,1,0:T(8,128)S(1)} %bitcast.47, f32[2,128,8,512]{3,2,1,0:T(8,128)S(1)} %copy-done.6), kind=kOutput, calls=%fused_computation.6 | convolution fusion | flops 3221225472 | bytes 7340032 | tf_op jit(solution)/shard_map/ickm,ickr->rim/dot_general | solution.py:36
  188.9 1.1 copy.53
  190.1 9.3 %reduce-scatter.5.cloned.1.call-done = f32[256,512]{1,0:T(8,128)} async-done(((f32[256,1024]{1,0:T(8,128)}), f32[256,512]{1,0:T(8,128)}) %reduce-scatter.5.cloned.1.call-update) | async-done | bytes 524304 | tf_op jit(solution)/shard_map/reduce_scatter | solution.py:40
  199.5 3.2 %fusion.9 = f32[256,512]{1,0:T(8,128)} fusion(f32[256,512]{1,0:T(8,128)} %reduce-scatter.5.cloned.1.call-done, f32[512,512]{1,0:T(8,128)S(1)} %copy-done, f32[256,1024]{1,0:T(8,128)} %all-gather.9.cloned.1.call-done, s32[]{:T(128)S(6)} %select_n.17, f32[256,1024]{1,0:T(8,128)} %param.7, s32[]{:T(128)S(6)} %select_n.15), kind=kOutput, calls=%fused_computation.13 | convolution fusion | flops 805568512 | bytes 3145736 | tf_op jit(solution)/shard_map/rb,mb->rm/dot_general | solution.py:39
  202.7 13.2 %all-gather.11.cloned.1.call-done = f32[256,1024]{1,0:T(8,128)} async-done(((f32[256,512]{1,0:T(8,128)}), f32[256,1024]{1,0:T(8,128)}) %all-gather.11.cloned.1.call-update) | async-done | bytes 1048592 | tf_op jit(solution)/shard_map/all_gather | solution.py:43
  215.9 2.9 %convolution_add_fusion = f32[256,512]{1,0:T(8,128)} fusion(f32[256,512]{1,0:T(8,128)S(1)} %copy-done.1, f32[512,512]{1,0:T(8,128)S(1)} %copy-done.3, f32[256,1024]{1,0:T(8,128)} %all-gather.11.cloned.1.call-done, s32[]{:T(128)S(6)} %select_n.17), kind=kOutput, calls=%fused_computation.8 | convolution fusion | flops 805437440 | bytes 2621444 | tf_op jit(solution)/shard_map/rb,mb->rm/dot_general | solution.py:47
  (23 shorter events, 0.3 us)
Async XLA Ops:
  7.2 89.5 %copy-start = (f32[512,512]{1,0:T(8,128)S(1)}, f32[512,512]{1,0:T(8,128)}, u32[]{:S(2)}) copy-start(f32[512,512]{1,0:T(8,128)} %param.12) | copy-start | bytes 3145732
  7.2 18.5 %all-gather.5.cloned.1.call-start = ((), (), s32[]{:S(2)}) async-start(), calls=%async_computation.4 | async-start | bytes 1572864 | tf_op jit(solution)/shard_map/all_gather | solution.py:31
  9.4 87.3 %reduce-scatter.3.cloned.1.call-start = ((), (), s32[]{:S(2)}) async-start(), calls=%async_computation.5 | async-start | bytes 1572864 | tf_op jit(solution)/shard_map/reduce_scatter | solution.py:40
  79.5 2.2 copy-start.5
  85.9 10.8 %copy-start.4 = (f32[256,1024]{0,1:T(8,128)S(1)}, f32[256,1024]{0,1:T(8,128)}, u32[]{:S(2)}) copy-start(f32[256,1024]{0,1:T(8,128)} %all-gather.5.cloned.1.call-done) | copy-start | bytes 3145732
  87.2 26.5 %copy-start.2 = (f32[512,512]{1,0:T(8,128)S(1)}, f32[512,512]{1,0:T(8,128)}, u32[]{:S(2)}) copy-start(f32[512,512]{1,0:T(8,128)} %param.13) | copy-start | bytes 3145732
  87.2 26.5 %all-gather.7.cloned.1.call-start = ((), (), s32[]{:S(2)}) async-start(), calls=%async_computation.6 | async-start | bytes 1572864 | tf_op jit(solution)/shard_map/all_gather | solution.py:43
  100.5 29.5 %all-gather.9.cloned.1.call-start = ((), (), s32[]{:S(2)}) async-start(), calls=%async_computation.7 | async-start | bytes 1572864 | tf_op jit(solution)/shard_map/all_gather | solution.py:31
  116.8 82.6 %reduce-scatter.5.cloned.1.call-start = ((), (), s32[]{:S(2)}) async-start(), calls=%async_computation.8 | async-start | bytes 1572864 | tf_op jit(solution)/shard_map/reduce_scatter | solution.py:40
  182.9 2.2 copy-start.6
  190.0 25.9 %copy-start.1 = (f32[256,512]{1,0:T(8,128)S(1)}, f32[256,512]{1,0:T(8,128)}, u32[]{:S(2)}) copy-start(f32[256,512]{1,0:T(8,128)} %convolution_add_fusion.2) | copy-start | bytes 1572868
  190.1 25.9 %copy-start.3 = (f32[512,512]{1,0:T(8,128)S(1)}, f32[512,512]{1,0:T(8,128)}, u32[]{:S(2)}) copy-start(f32[512,512]{1,0:T(8,128)} %param.13) | copy-start | bytes 3145732
  190.1 25.8 %all-gather.11.cloned.1.call-start = ((), (), s32[]{:S(2)}) async-start(), calls=%async_computation.9 | async-start | bytes 1572864 | tf_op jit(solution)/shard_map/all_gather | solution.py:43
Sparse Core Ops, SparseCore 0:
  10.2 15.3 all-gather.4
  87.3 9.2 reduce-scatter.2
  100.6 13.0 all-gather.6
  116.9 13.0 all-gather.8
  190.2 9.2 reduce-scatter.4
  202.8 13.0 all-gather.10
where the time goes:
time: 226 us
  blocking collectives  78.5 us (35%)
  waiting for transfers between devices  73.5 us (33%)
  matrix products  42.3 us (19%)
  local copies, waits for them, and re-layouts  15.8 us (7%)
  between operations  14.3 us (6%)
    all_to_all x2, blocking collectives, on_device(): lax.all_to_all(projected, 'row', split_axis=0, concat_axis=1, tiled=True)  78.5 us
    all_gather x2, waiting for transfers between devices, on_device(): guess_full = lax.all_gather(iterate_rows, 'pan', axis=1, tiled=True)  28.3 us
    all_gather x2, waiting for transfers between devices, on_device(): residual_full = lax.all_gather(residual, 'pan', axis=1, tiled=True)  26.4 us
    dot_general x2, matrix products, on_device(): jnp.einsum('cikb,rcb->ickr', v_factor, guess_tiles, precision=highest)  21.6 us
    reduce_scatter x2, waiting for transfers between devices, on_device(): lax.psum_scatter(low_rank, 'pan', scatter_dimension=1, tiled=True)  18.7 us
    dot_general x2, matrix products, on_device(): jnp.einsum('ickm,ickr->rim', u_factor, received, precision=highest)  7.64 us
    dot_general x2, matrix products, on_device(): jnp.einsum('rb,mb->rm', guess_tile, diag_block, precision=highest)  7.07 us
    unnamed x15, local copies, waits for them, and re-layouts  6.15 us
  transfers between devices with their start and end apart: 6, of which 6 were waited for; matrix products, arithmetic and copies ran while one was open for 0% of the time, Pallas kernels for 0%

commit v1 on v0

--- a/solution.py
+++ b/solution.py
@@ -32,7 +32,12 @@
         guess_tiles = guess_full.reshape(rhs_count, tile_rows, tile_width)
         projected = jnp.einsum("cikb,rcb->ickr", v_factor, guess_tiles, precision=highest)
         projected = projected * rank_mask[:, :, :, None]
-        received = lax.all_to_all(projected, "row", split_axis=0, concat_axis=1, tiled=True)
+        received = jnp.concatenate(
+            lax.all_to_all(
+                jnp.stack(jnp.split(projected, lax.axis_size("row"), axis=0)), "row", 0, 0
+            ),
+            axis=1,
+        )
         low_rank = jnp.einsum("ickm,ickr->rim", u_factor, received, precision=highest)
         low_rank = low_rank.reshape(rhs_count, tile_rows * tile_width)
         guess_tile = lax.dynamic_slice_in_dim(guess_full, tile_slot * tile_width, tile_width, 1)

time: 226 us -> 216 us (0.956)
  local copies, waits for them, and re-layouts: 15.8 us -> 9.94 us
  matrix products: 42.3 us -> 36.6 us
    dot_general x2, matrix products: 21.6 us -> 16.2 us  [on_device(): jnp.einsum('cikb,rcb->ickr', v_factor, guess_tiles, precision=highest)]
    mul x2 -> x0, local copies, waits for them, and re-layouts: 4.47 us -> none  [on_device(): projected = projected * rank_mask[:, :, :, None]]
    unnamed x15 -> x139, local copies, waits for them, and re-layouts: 6.15 us -> 5.02 us
where the time goes in v1:
time: 216 us; the launch traced here: 215 us
  blocking collectives  79 us (37%)
  waiting for transfers between devices  73.5 us (34%)
  matrix products  36.6 us (17%)
  between operations  14.9 us (7%)
  local copies, waits for them, and re-layouts  9.94 us (5%)
    all_to_all x2, blocking collectives, on_device(): lax.all_to_all(jnp.stack(jnp.split(projected, lax.axis_size('row'), axis=...  79 us
    all_gather x2, waiting for transfers between devices, on_device(): guess_full = lax.all_gather(iterate_rows, 'pan', axis=1, tiled=True)  28.6 us
    all_gather x2, waiting for transfers between devices, on_device(): residual_full = lax.all_gather(residual, 'pan', axis=1, tiled=True)  26.4 us
    reduce_scatter x2, waiting for transfers between devices, on_device(): lax.psum_scatter(low_rank, 'pan', scatter_dimension=1, tiled=True)  18.5 us
    dot_general x2, matrix products, on_device(): jnp.einsum('cikb,rcb->ickr', v_factor, guess_tiles, precision=highest)  16.2 us
    dot_general x2, matrix products, on_device(): jnp.einsum('ickm,ickr->rim', u_factor, received, precision=highest)  7.35 us
    dot_general x2, matrix products, on_device(): jnp.einsum('rb,mb->rm', guess_tile, diag_block, precision=highest)  7.07 us
    dot_general x2, matrix products, on_device(): jnp.einsum('rb,mb->rm', residual_tile, diag_inverse, precision=highest)  5.95 us
  transfers between devices with their start and end apart: 6, of which 6 were waited for; matrix products, arithmetic and copies ran while one was open for 0% of the time, Pallas kernels for 0%

profile of v1, /device:TPU:1, one launch (start us, length us, event | category | flops | bytes accessed | tf_op | source)
XLA Modules:
  0.0 215.3 jit_solution(12291600861220963867)
XLA Ops:
  7.2 0.0 all-gather.5.cloned.1.call-start
  7.2 2.1 copy.17
  9.4 0.0 reduce-scatter.3.cloned.1.call-start
  9.4 0.1 iota_compare_fusion
  9.5 0.8 and_convert_fusion
  10.3 15.4 %all-gather.5.cloned.1.call-done = f32[256,1024]{0,1:T(8,128)} async-done(((f32[256,512]{0,1:T(8,128)}), f32[256,1024]{0,1:T(8,128)}) %all-gather.5.cloned.1.call-update) | async-done | bytes 1048592 | tf_op jit(solution)/shard_map/all_gather | solution.py:31
  25.7 8.7 %bitcast_multiply_fusion.1 = f32[128,2,8,256]{3,0,2,1:T(8,128)S(1)} fusion(f32[256,2,512,1]{0,2,3,1:T(8,128)} %bitcast.551, f32[2,128,8,512]{3,2,1,0:T(8,128)} %param.9, f32[128,2,8]{0,2,1:T(8,128)S(1)} %and_convert_fusion), kind=kOutput, calls=%fused_computation.9 | convolution fusion | flops 3221749760 | bytes 7348224 | tf_op jit(solution)/shard_map/cikb,rcb->ickr/dot_general | solution.py:33
  36.1 39.5 %all_to_all.10 = f32[64,2,2,8,256]{4,1,3,2,0:T(2,128)S(1)} all-to-all(f32[64,2,2,8,256]{4,1,3,2,0:T(2,128)S(1)} %constant_dynamic-update-slice_fusion), channel_id=1, replica_groups=mesh['row'=64,'pan'=2] {'row'}, dimensions={0} | all-to-all | bytes 4194304 | tf_op jit(solution)/shard_map/all_to_all | solution.py:36
  75.7 3.7 %fusion.12 = f32[256,2,512]{2,0,1:T(8,128)S(1)} fusion(f32[2,128,8,512]{3,2,1,0:T(8,128)S(1)} %copy-done.4, f32[2,128,8,256]{3,0,2,1:T(2,128)S(1)} %bitcast.552), kind=kOutput, calls=%fused_computation.10 | convolution fusion | flops 3221225472 | bytes 7340032 | tf_op jit(solution)/shard_map/ickm,ickr->rim/dot_general | solution.py:41
  79.3 0.3 copy.22
  79.7 1.3 copy.23
  81.0 0.0 reduce-scatter.3.cloned.1.call-update
  81.1 0.2 all-gather.7.cloned.1.call-start
  81.3 9.2 %reduce-scatter.3.cloned.1.call-done = f32[256,512]{1,0:T(8,128)} async-done(((f32[256,1024]{1,0:T(8,128)}), f32[256,512]{1,0:T(8,128)}) %reduce-scatter.3.cloned.1.call-update) | async-done | bytes 524304 | tf_op jit(solution)/shard_map/reduce_scatter | solution.py:45
  90.5 3.9 %fusion.18 = f32[256,512]{1,0:T(8,128)} fusion(f32[256,512]{1,0:T(8,128)} %reduce-scatter.3.cloned.1.call-done, f32[512,512]{1,0:T(8,128)S(1)} %copy-done, f32[256,1024]{0,1:T(8,128)S(1)} %copy-done.3, s32[]{:T(128)S(6)} %select_n.17, f32[256,1024]{1,0:T(8,128)} %param.7, s32[]{:T(128)S(6)} %select_n.15), kind=kOutput, calls=%fused_computation.16 | convolution fusion | flops 805568512 | bytes 3145736 | tf_op jit(solution)/shard_map/rb,mb->rm/dot_general | solution.py:44
  94.3 0.0 all-gather.7.cloned.1.call-update
  94.3 0.0 all-gather.9.cloned.1.call-start
  94.4 13.2 %all-gather.7.cloned.1.call-done = f32[256,1024]{1,0:T(8,128)} async-done(((f32[256,512]{1,0:T(8,128)}), f32[256,1024]{1,0:T(8,128)}) %all-gather.7.cloned.1.call-update) | async-done | bytes 1048592 | tf_op jit(solution)/shard_map/all_gather | solution.py:48
  107.6 3.1 %convolution_add_fusion.2 = f32[256,512]{1,0:T(8,128)} fusion(f32[256,512]{1,0:T(8,128)} %param.8, f32[512,512]{1,0:T(8,128)S(1)} %copy-done.2, f32[256,1024]{1,0:T(8,128)} %all-gather.7.cloned.1.call-done, s32[]{:T(128)S(6)} %select_n.17), kind=kOutput, calls=%fused_computation.14 | convolution fusion | flops 805437440 | bytes 2621444 | tf_op jit(solution)/shard_map/rb,mb->rm/dot_general | solution.py:52
  110.6 0.0 reduce-scatter.5.cloned.1.call-start
  110.7 13.2 %all-gather.9.cloned.1.call-done = f32[256,1024]{1,0:T(8,128)} async-done(((f32[256,512]{1,0:T(8,128)}), f32[256,1024]{1,0:T(8,128)}) %all-gather.9.cloned.1.call-update) | async-done | bytes 1048592 | tf_op jit(solution)/shard_map/all_gather | solution.py:31
  123.9 2.1 reshape.63
  126.0 7.6 %bitcast_multiply_fusion = f32[128,2,8,256]{3,0,2,1:T(8,128)S(1)} fusion(f32[2,128,8,512]{3,2,1,0:T(8,128)} %param.9, f32[256,2,512,1]{2,1,0,3:T(2,128)S(1)} %bitcast.550, f32[128,2,8]{0,2,1:T(8,128)S(1)} %and_convert_fusion), kind=kOutput, calls=%fused_computation.6 | convolution fusion | flops 3221749760 | bytes 7348224 | tf_op jit(solution)/shard_map/cikb,rcb->ickr/dot_general | solution.py:33
  135.4 39.5 %all_to_all.11 = f32[64,2,2,8,256]{4,1,3,2,0:T(2,128)S(1)} all-to-all(f32[64,2,2,8,256]{4,1,3,2,0:T(2,128)S(1)} %constant_dynamic-update-slice_fusion.64), channel_id=1, replica_groups=mesh['row'=64,'pan'=2] {'row'}, dimensions={0} | all-to-all | bytes 4194304 | tf_op jit(solution)/shard_map/all_to_all | solution.py:36
  174.9 3.7 %fusion.15 = f32[2,32,8,512]{3,2,1,0:T(8,128)S(1)} fusion(f32[2,128,8,512]{3,2,1,0:T(8,128)S(1)} %copy-done.5, f32[2,128,8,256]{3,0,2,1:T(2,128)S(1)} %bitcast.553), kind=kOutput, calls=%fused_computation.11 | convolution fusion | flops 3221225472 | bytes 7340032 | tf_op jit(solution)/shard_map/ickm,ickr->rim/dot_general | solution.py:41
  178.6 1.1 copy.43
  179.7 0.0 reduce-scatter.5.cloned.1.call-update
  179.7 0.0 all-gather.11.cloned.1.call-start
  179.8 9.3 %reduce-scatter.5.cloned.1.call-done = f32[256,512]{1,0:T(8,128)} async-done(((f32[256,1024]{1,0:T(8,128)}), f32[256,512]{1,0:T(8,128)}) %reduce-scatter.5.cloned.1.call-update) | async-done | bytes 524304 | tf_op jit(solution)/shard_map/reduce_scatter | solution.py:45
  189.1 3.2 %fusion.19 = f32[256,512]{1,0:T(8,128)} fusion(f32[256,512]{1,0:T(8,128)} %reduce-scatter.5.cloned.1.call-done, f32[512,512]{1,0:T(8,128)S(1)} %copy-done, f32[256,1024]{1,0:T(8,128)} %all-gather.9.cloned.1.call-done, s32[]{:T(128)S(6)} %select_n.17, f32[256,1024]{1,0:T(8,128)} %param.7, s32[]{:T(128)S(6)} %select_n.15), kind=kOutput, calls=%fused_computation.17 | convolution fusion | flops 805568512 | bytes 3145736 | tf_op jit(solution)/shard_map/rb,mb->rm/dot_general | solution.py:44
  192.3 13.2 %all-gather.11.cloned.1.call-done = f32[256,1024]{1,0:T(8,128)} async-done(((f32[256,512]{1,0:T(8,128)}), f32[256,1024]{1,0:T(8,128)}) %all-gather.11.cloned.1.call-update) | async-done | bytes 1048592 | tf_op jit(solution)/shard_map/all_gather | solution.py:48
  205.5 2.9 %convolution_add_fusion = f32[256,512]{1,0:T(8,128)} fusion(f32[256,512]{1,0:T(8,128)S(1)} %copy-done.1, f32[512,512]{1,0:T(8,128)S(1)} %copy-done.2, f32[256,1024]{1,0:T(8,128)} %all-gather.11.cloned.1.call-done, s32[]{:T(128)S(6)} %select_n.17), kind=kOutput, calls=%fused_computation.12 | convolution fusion | flops 805437440 | bytes 2621444 | tf_op jit(solution)/shard_map/rb,mb->rm/dot_general | solution.py:52
  (145 shorter events, 3.0 us)
Async XLA Ops:
  7.2 83.3 %copy-start = (f32[512,512]{1,0:T(8,128)S(1)}, f32[512,512]{1,0:T(8,128)}, u32[]{:S(2)}) copy-start(f32[512,512]{1,0:T(8,128)} %param.12) | copy-start | bytes 3145732
  7.2 18.5 %all-gather.5.cloned.1.call-start = ((), (), s32[]{:S(2)}) async-start(), calls=%async_computation.4 | async-start | bytes 1572864 | tf_op jit(solution)/shard_map/all_gather | solution.py:31
  9.4 81.1 %reduce-scatter.3.cloned.1.call-start = ((), (), s32[]{:S(2)}) async-start(), calls=%async_computation.5 | async-start | bytes 1572864 | tf_op jit(solution)/shard_map/reduce_scatter | solution.py:45
  36.1 39.5 %copy-start.4 = (f32[2,128,8,512]{3,2,1,0:T(8,128)S(1)}, f32[2,128,8,512]{3,2,1,0:T(8,128)}, u32[]{:S(2)}) copy-start(f32[2,128,8,512]{3,2,1,0:T(8,128)} %param.10) | copy-start | bytes 12582916
  79.7 10.8 %copy-start.3 = (f32[256,1024]{0,1:T(8,128)S(1)}, f32[256,1024]{0,1:T(8,128)}, u32[]{:S(2)}) copy-start(f32[256,1024]{0,1:T(8,128)} %all-gather.5.cloned.1.call-done) | copy-start | bytes 3145732
  81.0 26.5 %copy-start.2 = (f32[512,512]{1,0:T(8,128)S(1)}, f32[512,512]{1,0:T(8,128)}, u32[]{:S(2)}) copy-start(f32[512,512]{1,0:T(8,128)} %param.13) | copy-start | bytes 3145732
  81.1 26.5 %all-gather.7.cloned.1.call-start = ((), (), s32[]{:S(2)}) async-start(), calls=%async_computation.6 | async-start | bytes 1572864 | tf_op jit(solution)/shard_map/all_gather | solution.py:48
  94.3 29.5 %all-gather.9.cloned.1.call-start = ((), (), s32[]{:S(2)}) async-start(), calls=%async_computation.7 | async-start | bytes 1572864 | tf_op jit(solution)/shard_map/all_gather | solution.py:31
  110.6 78.5 %reduce-scatter.5.cloned.1.call-start = ((), (), s32[]{:S(2)}) async-start(), calls=%async_computation.8 | async-start | bytes 1572864 | tf_op jit(solution)/shard_map/reduce_scatter | solution.py:45
  135.4 39.5 %copy-start.5 = (f32[2,128,8,512]{3,2,1,0:T(8,128)S(1)}, f32[2,128,8,512]{3,2,1,0:T(8,128)}, u32[]{:S(2)}) copy-start(f32[2,128,8,512]{3,2,1,0:T(8,128)} %param.10) | copy-start | bytes 12582916
  179.7 25.9 %copy-start.1 = (f32[256,512]{1,0:T(8,128)S(1)}, f32[256,512]{1,0:T(8,128)}, u32[]{:S(2)}) copy-start(f32[256,512]{1,0:T(8,128)} %convolution_add_fusion.2) | copy-start | bytes 1572868
  179.7 25.8 %all-gather.11.cloned.1.call-start = ((), (), s32[]{:S(2)}) async-start(), calls=%async_computation.9 | async-start | bytes 1572864 | tf_op jit(solution)/shard_map/all_gather | solution.py:48
Sparse Core Ops, SparseCore 0:
  10.2 15.3 all-gather.4
  81.2 9.2 reduce-scatter.2
  94.5 13.0 all-gather.6
  110.8 13.0 all-gather.8
  179.8 9.2 reduce-scatter.4
  192.5 13.0 all-gather.10
